TPU v7x, 32 devices: a whole 2x2x4 slice. The times are simulated.
32 devices in a mesh: dp: 4 (over z), tensor: 8 (over y, x, core).
Axes of the slice: x: 2, y: 2, z: 4, core: 2. Of those that a mesh axis runs over, the one named last changes fastest.
Arguments:
- hidden_in: bfloat16 [4, 1024, 2304], P('dp', 'tensor'), may hold values from -6 to 6
- prompt_len: int32 [4], P('dp'), may hold values from 1 to 1024, 2560 in all
- start_pos: int32 [4], P('dp'), may hold values from 0 to 511
- routes: int32 [4, 1024, 2], P('dp'), may hold values from 0 to 7, as said below
- trainer_qkv: float32 [2304, 3, 2048], P(('tensor', 'dp')), may hold values from -1 to 1
- trainer_out: float32 [2048, 2304], P(('tensor', 'dp')), may hold values from -0.125 to 0.125
- trainer_gate: float32 [2304, 5760], P('tensor'), may hold values from -0.125 to 0.125
- trainer_up: float32 [2304, 5760], P('tensor'), may hold values from -0.125 to 0.125
- trainer_down: float32 [2304, 5760], P('tensor'), may hold values from -0.078125 to 0.078125
- attn_gain: float32 [2304], replicated, may hold values from 0.25 to 1.75
- moe_gain: float32 [2304], replicated, may hold values from 0.25 to 1.75
- router: bfloat16 [2304, 8], replicated, may hold values from -0.125 to 0.125
Outputs:
- server_qkv: bfloat16 [2304, 3, 2048], P(None, None, 'tensor')
- server_out: bfloat16 [2048, 2304], P('tensor')
- server_gate: bfloat16 [2304, 5760], P(None, 'tensor')
- server_up: bfloat16 [2304, 5760], P(None, 'tensor')
- server_down: bfloat16 [2304, 5760], P(None, 'tensor')
- hidden_out: bfloat16 [4, 1024, 2304], P('dp', 'tensor')
- kv_cache: bfloat16 [4, 2, 1024, 2048], P('dp', None, None, 'tensor')
Inputs may be any that keep to these rules, and one draw needn't show every extreme that they name: `routes`: each row names two different experts; expert 0 is named by at most 512 rows of each prompt and by exactly 512 rows of some prompt.
All inputs are finite; a program needn't handle non-finite values. No bound on the sum of `prompt_len` on one device may be relied on, other than what follows from the above.
Results may differ from a plain program's by a relative error of at most 0.011.
The roundings to bfloat16 on the way count: a program that leaves them out, or rounds other values in their place, can miss the bound.
Values may be sent and summed in bfloat16 or wider, within the bound.
No kernel may reach another device: no remote copies, remote signals or barrier semaphores. Data moves between devices by JAX's collectives and lax.ppermute only.
A program may use at most 256 MiB of HBM per device.

v0:
```python
import jax
import jax.numpy as jnp
from jax import lax
from jax.sharding import PartitionSpec as P

HEAD_DIM = 64


def rms_scale(values, gain_row):
    mean_sq = jnp.mean(values * values, axis=-1, keepdims=True)
    return values * lax.rsqrt(mean_sq + 1e-05) * gain_row


def rotate(head_block, positions):
    half_dim = head_block.shape[-1] // 2
    inv_freq = jnp.power(
        10000.0, jnp.arange(half_dim, dtype=jnp.float32) * (-2.0 / head_block.shape[-1])
    )
    angles = positions.astype(jnp.float32)[:, None] * inv_freq[None, :]
    cosine = jnp.cos(angles)[:, None, :]
    sine_part = jnp.sin(angles)[:, None, :]
    first_half = head_block[..., :half_dim]
    second_half = head_block[..., half_dim:]
    return jnp.concatenate(
        [
            first_half * cosine - second_half * sine_part,
            second_half * cosine + first_half * sine_part,
        ],
        axis=-1,
    )


def attend_block(query_blk, key_blk, value_blk, row_start):
    scores = jnp.einsum(
        "qhd,khd->hqk", query_blk, key_blk, preferred_element_type=jnp.float32
    ) * query_blk.shape[-1] ** (-0.5)
    row_ids = row_start + jnp.arange(query_blk.shape[0], dtype=jnp.int32)
    col_ids = jnp.arange(key_blk.shape[0], dtype=jnp.int32)
    scores = jnp.where(row_ids[None, :, None] >= col_ids[None, None, :], scores, -1e30)
    row_max = jnp.max(scores, axis=-1, keepdims=True)
    exp_scores = jnp.exp(scores - row_max)
    attn_probs = (exp_scores / jnp.sum(exp_scores, axis=-1, keepdims=True)).astype(jnp.bfloat16)
    return jnp.einsum(
        "hqk,khd->qhd", attn_probs, value_blk, preferred_element_type=jnp.float32
    ).astype(jnp.bfloat16)


def shards(
    hidden_in,
    prompt_len,
    start_pos,
    routes,
    trainer_qkv,
    trainer_out,
    trainer_gate,
    trainer_up,
    trainer_down,
    attn_gain,
    moe_gain,
    router,
):
    tensor_size = lax.axis_size("tensor")
    replica_count = lax.axis_size("dp")
    expert_mats = (
        lax.all_to_all(
            trainer_gate.astype(jnp.bfloat16), "tensor", split_axis=1, concat_axis=0, tiled=True
        ),
        lax.all_to_all(
            trainer_up.astype(jnp.bfloat16), "tensor", split_axis=1, concat_axis=0, tiled=True
        ),
        lax.all_to_all(
            trainer_down.astype(jnp.bfloat16), "tensor", split_axis=1, concat_axis=0, tiled=True
        ),
    )
    server_gate, server_up, server_down = expert_mats
    qkv_cast = trainer_qkv.astype(jnp.bfloat16)
    out_cast = trainer_out.astype(jnp.bfloat16)
    column_part = lax.all_to_all(qkv_cast, "tensor", split_axis=2, concat_axis=0, tiled=True)
    stacked, server_out = (
        lax.all_gather(column_part, "dp", axis=0, tiled=True),
        lax.all_gather(out_cast, "dp", axis=0, tiled=True),
    )
    block_rows = stacked.shape[0] // (replica_count * tensor_size)
    server_qkv = (
        stacked.reshape(replica_count, tensor_size, block_rows, 3, stacked.shape[2])
        .transpose(1, 0, 2, 3, 4)
        .reshape(stacked.shape)
    )
    rows_dev = hidden_in.shape[1]
    seq_len = rows_dev * tensor_size
    length = prompt_len[0]
    offset = start_pos[0]
    my_first = lax.axis_index("tensor") * rows_dev
    tokens = hidden_in[0].astype(jnp.float32)
    normed = rms_scale(tokens, attn_gain).astype(jnp.bfloat16)
    local_width = server_qkv.shape[2]
    heads_here = local_width // HEAD_DIM
    piece = lax.all_gather(normed, "tensor", axis=0, tiled=True)
    mixed = jnp.einsum("sd,dtc->stc", piece, server_qkv, preferred_element_type=jnp.float32)
    places = offset + jnp.arange(piece.shape[0], dtype=jnp.int32)
    query_rot = rotate(mixed[:, 0].reshape(-1, heads_here, HEAD_DIM), places).reshape(
        -1, local_width
    )
    key_rot = rotate(mixed[:, 1].reshape(-1, heads_here, HEAD_DIM), places).reshape(-1, local_width)
    qkv_rows = jnp.stack([query_rot, key_rot, mixed[:, 2]], axis=1).astype(jnp.bfloat16)
    query_all = qkv_rows[:, 0].reshape(seq_len, heads_here, HEAD_DIM)
    keys_all = qkv_rows[:, 1].reshape(seq_len, heads_here, HEAD_DIM)
    values_all = qkv_rows[:, 2].reshape(seq_len, heads_here, HEAD_DIM)
    block_len = min(512, seq_len)
    block_outs = []
    for block_id in range(seq_len // block_len):
        row_lo = block_id * block_len
        row_hi = row_lo + block_len
        query_blk = query_all[row_lo:row_hi]
        key_blk = keys_all[:row_hi]
        value_blk = values_all[:row_hi]
        block_result = attend_block(query_blk, key_blk, value_blk, row_lo)
        block_outs.append(block_result)
    attended = jnp.concatenate(block_outs, axis=0).reshape(seq_len, local_width)
    attn_sum = lax.psum_scatter(
        jnp.dot(attended, server_out, preferred_element_type=jnp.float32).astype(jnp.bfloat16),
        "tensor",
        scatter_dimension=0,
        tiled=True,
    ).astype(jnp.float32)
    middle = (tokens + attn_sum).astype(jnp.bfloat16)
    normed_moe = rms_scale(middle.astype(jnp.float32), moe_gain).astype(jnp.bfloat16)
    local_routes = lax.dynamic_slice_in_dim(routes[0], my_first, rows_dev, 0)
    local_valid = my_first + jnp.arange(rows_dev, dtype=jnp.int32) < length
    logits = jnp.dot(normed_moe, router, preferred_element_type=jnp.float32)
    expert_ids = jnp.arange(router.shape[1], dtype=jnp.int32)
    logit_first = jnp.sum(
        jnp.where(local_routes[:, 0:1] == expert_ids[None, :], logits, 0.0), axis=1
    )
    logit_second = jnp.sum(
        jnp.where(local_routes[:, 1:2] == expert_ids[None, :], logits, 0.0), axis=1
    )
    other_logit = jnp.where(local_routes[:, 0] == 0, logit_second, logit_first)
    local_routed = jnp.any(local_routes == 0, axis=1)
    route_w = jnp.where(local_routed, jax.nn.sigmoid(logits[:, 0] - other_logit), 0.0)
    gathered = lax.all_gather(normed_moe, "tensor", axis=0, tiled=True)
    seq_ids = jnp.arange(seq_len, dtype=jnp.int32)
    all_routed = jnp.any(routes[0] == 0, axis=1)
    capacity = seq_len // 2
    slot = jnp.cumsum(all_routed.astype(jnp.int32)) - 1
    slot_rows = (
        jnp.full((capacity,), seq_len, jnp.int32)
        .at[jnp.where(all_routed, slot, capacity)]
        .set(seq_ids, mode="drop")
    )
    picked = gathered[jnp.minimum(slot_rows, seq_len - 1)]
    gate_val = jnp.dot(picked, server_gate, preferred_element_type=jnp.float32)
    up_val = jnp.dot(picked, server_up, preferred_element_type=jnp.float32)
    act = (jax.nn.silu(gate_val) * up_val).astype(jnp.bfloat16)
    slot_sums = lax.dot_general(
        act, server_down, (((1,), (1,)), ((), ())), preferred_element_type=jnp.float32
    )
    terms = (
        jnp.zeros((seq_len, normed_moe.shape[1]), jnp.float32)
        .at[slot_rows]
        .add(slot_sums, mode="drop")
    )
    expert_sum = lax.psum_scatter(
        terms.astype(jnp.bfloat16), "tensor", scatter_dimension=0, tiled=True
    ).astype(jnp.float32)
    result = middle.astype(jnp.float32) + route_w[:, None] * expert_sum
    hidden_out = jnp.where(local_valid[:, None], result, 0.0).astype(jnp.bfloat16)[None]
    seq_valid = jnp.arange(seq_len, dtype=jnp.int32) < length
    cache_pair = jnp.where(
        seq_valid[None, :, None], qkv_rows[:, 1:3].transpose(1, 0, 2), jnp.zeros((), jnp.bfloat16)
    )
    return (
        server_qkv,
        server_out,
        server_gate,
        server_up,
        server_down,
        hidden_out,
        cache_pair[None],
    )


def solution(mesh):
    placed = (
        P("dp", "tensor", None),
        P("dp"),
        P("dp"),
        P("dp", None, None),
        P(("tensor", "dp"), None, None),
        P(("tensor", "dp"), None),
        P("tensor", None),
        P("tensor", None),
        P("tensor", None),
        P(),
        P(),
        P(),
    )
    return jax.shard_map(
        shards,
        mesh=mesh,
        in_specs=placed,
        out_specs=(
            P(None, None, "tensor"),
            P("tensor", None),
            P(None, "tensor"),
            P(None, "tensor"),
            P(None, "tensor"),
            P("dp", "tensor", None),
            P("dp", None, None, "tensor"),
        ),
        check_vma=False,
    )
```

profile of v0, /device:TPU:0, one launch (start us, length us, event | category | flops | bytes accessed | tf_op | source)
XLA Modules:
  0.0 508.5 jit_solution(11771919291552511364)
XLA Ops:
  7.2 2.5 convert_element_type.86
  9.7 2.9 copy.59
  12.6 3.7 reshape.272
  16.3 18.9 %all_to_all.75 = bf16[8,2,27648]{2,1,0:T(2,128)(2,1)} all-to-all(bf16[8,2,27648]{2,1,0:T(2,128)(2,1)} %reshape.272), channel_id=1, replica_groups=mesh['dp'=4,'tensor'=8] {'tensor'}, dimensions={0} | all-to-all | bytes 1769472 | tf_op jit(solution)/shard_map/all_to_all | solution.py:78
  35.2 4.5 reshape.273
  39.7 2.2 copy.75
  46.1 65.7 %all-gather.5.cloned.1.call-done = bf16[2304,3,256]{2,0,1:T(8,128)(2,1)} async-done(((bf16[576,3,256]{2,0,1:T(8,128)(2,1)}), bf16[2304,3,256]{2,0,1:T(8,128)(2,1)}) %all-gather.5.cloned.1.call-update) | async-done | bytes 3538960 | tf_op jit(solution)/shard_map/all_gather | solution.py:80
  111.8 4.2 copy.62
  115.9 35.8 %all-gather.9.cloned.1.call-done = bf16[1024,2304]{1,0:T(8,128)(2,1)} async-done(((bf16[128,2304]{1,0:T(8,128)(2,1)}), bf16[1024,2304]{1,0:T(8,128)(2,1)}) %all-gather.9.cloned.1.call-update) | async-done | bytes 4718608 | tf_op jit(solution)/shard_map/all_gather | solution.py:98
  151.8 6.8 %fusion.61 = (bf16[1024,3,256]{0,2,1:T(8,128)(2,1)S(1)}, f32[1024,3,256]{0,2,1:T(8,128)S(1)}) fusion(bf16[2304,3,256]{2,0,1:T(8,128)(2,1)} %bitcast.102, bf16[1024,2304]{1,0:T(8,128)(2,1)} %all-gather.9.cloned.1.call-done), kind=kOutput, calls=%fused_computation.108 | convolution fusion | flops 3624665088 | bytes 12976128 | tf_op jit(solution)/shard_map/sd,dtc->stc/dot_general | solution.py:99
  159.2 5.4 %fusion.62 = (f32[4,512]{1,0:T(4,128)S(1)}, f32[4,512,1024]{2,1,0:T(8,128)}) fusion(pred[512,1024]{1,0:T(8,128)(4,1)S(1)} %iota_compare_fusion, bf16[1024,4,32]{0,2,1:T(8,128)(2,1)S(1)} %get-tuple-element.52, bf16[1024,4,32]{0,2,1:T(8,128)(2,1)S(1)} %get-tuple-element.53, bf16[1024,4,32]{0,2,1:T(8,128)(2,1)S(1)} %get-tuple-element.49, ...), kind=kOutput, calls=%fused_computation.109 | convolution fusion | flops 278397952 | bytes 9969664 | tf_op jit(solution)/shard_map/sub | solution.py:41
  164.6 3.7 fusion.63
  168.2 2.9 fusion.28
  171.1 1.8 copy-done.13
  172.9 1.5 fusion.27
  174.5 10.0 %all-gather.7.cloned.1.call-done = bf16[256,2304]{1,0:T(8,128)(2,1)} async-done(((bf16[64,2304]{1,0:T(8,128)(2,1)}), bf16[256,2304]{1,0:T(8,128)(2,1)}) %all-gather.7.cloned.1.call-update) | async-done | bytes 1179664 | tf_op jit(solution)/shard_map/all_gather | solution.py:81
  184.4 4.8 convolution_convert_fusion
  189.9 52.6 %reduce-scatter.3.cloned.1.call-done = bf16[128,2304]{1,0:T(8,128)(2,1)} async-done(((bf16[1024,2304]{1,0:T(8,128)(2,1)}), bf16[128,2304]{1,0:T(8,128)(2,1)}) %reduce-scatter.3.cloned.1.call-update) | async-done | bytes 589840 | tf_op jit(solution)/shard_map/reduce_scatter | solution.py:120
  242.4 1.3 fusion.18
  243.8 2.1 fusion.20
  246.0 4.9 convert_element_type.88
  250.9 8.5 %all_to_all.59 = bf16[288,8,720]{2,1,0:T(8,128)(2,1)} reshape(bf16[288,5760]{1,0:T(8,128)(2,1)} %convert_element_type.88) | data formatting | bytes 6635520 | tf_op jit(solution)/shard_map/all_to_all | solution.py:65
  259.4 4.6 copy.63
  264.0 4.5 all-to-all-start.1
  268.4 5.0 convert_element_type.89
  273.4 8.5 %all_to_all.63 = bf16[288,8,720]{2,1,0:T(8,128)(2,1)} reshape(bf16[288,5760]{1,0:T(8,128)(2,1)} %convert_element_type.89) | data formatting | bytes 6635520 | tf_op jit(solution)/shard_map/all_to_all | solution.py:68
  281.9 4.4 copy.64
  286.4 35.8 %all-to-all-done.1 = bf16[288,8,720]{2,0,1:T(8,128)(2,1)} async-done(((bf16[288,8,720]{2,0,1:T(8,128)(2,1)}), bf16[288,8,720]{2,0,1:T(8,128)(2,1)}, u32[]{:S(2)}, u32[]{:S(2)}) %all-to-all-start.1) | async-done | bytes 3317792 | tf_op jit(solution)/shard_map/all_to_all | solution.py:65
  322.2 4.5 all-to-all-start.2
  326.7 4.9 convert_element_type.90
  331.6 8.4 %all_to_all.67 = bf16[288,8,720]{2,1,0:T(8,128)(2,1)} reshape(bf16[288,5760]{1,0:T(8,128)(2,1)} %convert_element_type.90) | data formatting | bytes 6635520 | tf_op jit(solution)/shard_map/all_to_all | solution.py:71
  340.1 4.6 copy.65
  344.6 24.2 %all-to-all-done.2 = bf16[288,8,720]{2,0,1:T(8,128)(2,1)} async-done(((bf16[288,8,720]{2,0,1:T(8,128)(2,1)}), bf16[288,8,720]{2,0,1:T(8,128)(2,1)}, u32[]{:S(2)}, u32[]{:S(2)}) %all-to-all-start.2) | async-done | bytes 3317792 | tf_op jit(solution)/shard_map/all_to_all | solution.py:68
  368.8 4.5 all-to-all-start.3
  374.0 4.5 scatter_custom_fusion
  378.5 7.8 %gather_fusion = bf16[512,2304]{1,0:T(8,128)(2,1)S(1)} fusion(bf16[1024,2304]{1,0:T(8,128)(2,1)} %all-gather.11.cloned.1.call-done, s32[1024]{0:T(1024)S(1)} %pad_clamp_fusion), kind=kCustom, calls=%fused_computation | custom fusion | bytes 4720640 | tf_op jit(solution)/shard_map/gather | solution.py:151
  386.4 5.0 fusion.72
  391.4 24.0 %all-to-all-done.3 = bf16[288,8,720]{2,0,1:T(8,128)(2,1)} async-done(((bf16[288,8,720]{2,0,1:T(8,128)(2,1)}), bf16[288,8,720]{2,0,1:T(8,128)(2,1)}, u32[]{:S(2)}, u32[]{:S(2)}) %all-to-all-start.3) | async-done | bytes 3317792 | tf_op jit(solution)/shard_map/all_to_all | solution.py:71
  415.4 9.9 %fusion.32 = f32[512,2304]{1,0:T(8,128)} fusion(bf16[2304,720]{1,0:T(8,128)(2,1)} %bitcast.12, f32[512,720]{0,1:T(8,128)} %fusion.72, bf16[512,2304]{1,0:T(8,128)(2,1)S(1)} %gather_fusion, bf16[2304,720]{1,0:T(8,128)(2,1)} %bitcast.10), kind=kOutput, calls=%fused_computation.51 | convolution fusion | flops 3399598080 | bytes 15187968 | tf_op jit(solution)/shard_map/dot_general | solution.py:155
  425.3 13.3 %scatter_custom_fusion.1 = f32[1024,2304]{1,0:T(8,128)} fusion(s32[512]{0:T(512)S(1)} %get-tuple-element.57, f32[512,2304]{1,0:T(8,128)} %fusion.32, f32[]{:T(128)} %constant.20.clone.1), kind=kCustom, calls=%fused_computation.12 | custom fusion | flops 1179648 | bytes 9437696 | tf_op jit(solution)/shard_map/scatter-add | solution.py:161
  438.6 6.4 %convert_element_type.109 = bf16[1024,2304]{1,0:T(8,128)(2,1)} convert(f32[1024,2304]{1,0:T(8,128)} %scatter_custom_fusion.1) | non-fusion elementwise | flops 2359296 | bytes 14155776 | tf_op jit(solution)/shard_map/convert_element_type | solution.py:164
  445.7 5.7 %copy.68 = bf16[2304,720]{0,1:T(8,128)(2,1)} copy(bf16[2304,720]{1,0:T(8,128)(2,1)} %bitcast.8) | data formatting | bytes 6635520
  451.4 5.9 %copy.69 = bf16[2304,720]{0,1:T(8,128)(2,1)} copy(bf16[2304,720]{1,0:T(8,128)(2,1)} %bitcast.10) | data formatting | bytes 6635520
  457.3 5.7 %copy.70 = bf16[2304,720]{0,1:T(8,128)(2,1)} copy(bf16[2304,720]{1,0:T(8,128)(2,1)} %bitcast.12) | data formatting | bytes 6635520
  463.2 1.1 fusion.29
  464.2 2.3 copy.71
  466.8 31.4 %reduce-scatter.5.cloned.1.call-done = bf16[128,2304]{1,0:T(8,128)(2,1)} async-done(((bf16[1024,2304]{1,0:T(8,128)(2,1)}), bf16[128,2304]{1,0:T(8,128)(2,1)}) %reduce-scatter.5.cloned.1.call-update) | async-done | bytes 589840 | tf_op jit(solution)/shard_map/reduce_scatter | solution.py:163
  498.2 2.2 fusion.33
  (75 shorter events, 6.8 us)
Async XLA Ops:
  7.2 459.3 %copy-start = (bf16[2304,8]{0,1:T(8,128)(2,1)S(1)}, bf16[2304,8]{0,1:T(8,128)(2,1)}, u32[]{:S(2)}) copy-start(bf16[2304,8]{0,1:T(8,128)(2,1)} %param.23) | copy-start | bytes 110596
  7.2 104.6 %all-gather.5.cloned.1.call-start = ((), (), s32[]{:S(2)}) async-start(), calls=%async_computation.6 | async-start | bytes 4423680 | tf_op jit(solution)/shard_map/all_gather | solution.py:80
  35.2 6.8 %copy-start.1 = (bf16[1,128,2304]{2,1,0:T(8,128)(2,1)S(1)}, bf16[1,128,2304]{2,1,0:T(8,128)(2,1)}, u32[]{:S(2)}) copy-start(bf16[1,128,2304]{2,1,0:T(8,128)(2,1)} %param.12) | copy-start | bytes 1769476
  35.2 7.0 %copy-start.10 = (f32[2304]{0:T(1024)S(1)}, f32[2304]{0:T(1024)}, u32[]{:S(2)}) copy-start(f32[2304]{0:T(1024)} %param.21) | copy-start | bytes 27652
  39.7 3.6 copy-start.9
  41.9 109.9 %all-gather.9.cloned.1.call-start = ((), (), s32[]{:S(2)}) async-start(), calls=%async_computation.8 | async-start | bytes 5308416 | tf_op jit(solution)/shard_map/all_gather | solution.py:98
  43.2 141.2 %all-gather.7.cloned.1.call-start = ((), (), s32[]{:S(2)}) async-start(), calls=%async_computation.7 | async-start | bytes 1474560 | tf_op jit(solution)/shard_map/all_gather | solution.py:81
  44.1 198.4 %reduce-scatter.3.cloned.1.call-start = ((), (), s32[]{:S(2)}) async-start(), calls=%async_computation.9 | async-start | bytes 5308416 | tf_op jit(solution)/shard_map/reduce_scatter | solution.py:120
  159.2 5.4 %copy-start.5 = (bf16[1024,4,32]{0,2,1:T(8,128)(2,1)}, bf16[1024,4,32]{0,2,1:T(8,128)(2,1)S(1)}, u32[]{:S(2)}) copy-start(bf16[1024,4,32]{0,2,1:T(8,128)(2,1)S(1)} %get-tuple-element.48) | copy-start | bytes 786436
  159.2 5.4 %copy-start.7 = (bf16[1024,4,32]{0,2,1:T(8,128)(2,1)}, bf16[1024,4,32]{0,2,1:T(8,128)(2,1)S(1)}, u32[]{:S(2)}) copy-start(bf16[1024,4,32]{0,2,1:T(8,128)(2,1)S(1)} %get-tuple-element.49) | copy-start | bytes 786436
  168.2 4.7 copy-start.13
  189.3 54.5 %copy-start.11 = (f32[2304]{0:T(1024)S(1)}, f32[2304]{0:T(1024)}, u32[]{:S(2)}) copy-start(f32[2304]{0:T(1024)} %param.22) | copy-start | bytes 27652
  189.3 189.2 %all-gather.11.cloned.1.call-start = ((), (), s32[]{:S(2)}) async-start(), calls=%async_computation.10 | async-start | bytes 5308416 | tf_op jit(solution)/shard_map/all_gather | solution.py:141
  264.0 58.2 %all-to-all-start.1 = ((bf16[288,8,720]{2,0,1:T(8,128)(2,1)}), bf16[288,8,720]{2,0,1:T(8,128)(2,1)}, u32[]{:S(2)}, u32[]{:S(2)}) async-start(bf16[288,8,720]{2,0,1:T(8,128)(2,1)} %copy.63), calls=%async_computation.1 | async-start | bytes 7077888 | tf_op jit(solution)/shard_map/all_to_all | solution.py:65
  322.2 46.6 %all-to-all-start.2 = ((bf16[288,8,720]{2,0,1:T(8,128)(2,1)}), bf16[288,8,720]{2,0,1:T(8,128)(2,1)}, u32[]{:S(2)}, u32[]{:S(2)}) async-start(bf16[288,8,720]{2,0,1:T(8,128)(2,1)} %copy.64), calls=%async_computation.2 | async-start | bytes 7077888 | tf_op jit(solution)/shard_map/all_to_all | solution.py:68
  344.6 28.7 %copy-start.12 = (s32[1,1024,2]{1,2,0:T(2,128)S(1)}, s32[1,1024,2]{1,2,0:T(2,128)}, u32[]{:S(2)}) copy-start(s32[1,1024,2]{1,2,0:T(2,128)} %param.15) | copy-start | bytes 24580
  368.8 46.6 %all-to-all-start.3 = ((bf16[288,8,720]{2,0,1:T(8,128)(2,1)}), bf16[288,8,720]{2,0,1:T(8,128)(2,1)}, u32[]{:S(2)}, u32[]{:S(2)}) async-start(bf16[288,8,720]{2,0,1:T(8,128)(2,1)} %copy.65), calls=%async_computation.3 | async-start | bytes 7077888 | tf_op jit(solution)/shard_map/all_to_all | solution.py:71
  373.3 124.9 %reduce-scatter.5.cloned.1.call-start = ((), (), s32[]{:S(2)}) async-start(), calls=%async_computation.11 | async-start | bytes 5308416 | tf_op jit(solution)/shard_map/reduce_scatter | solution.py:163
  457.3 5.7 %copy-start.6 = (bf16[1024,4,32]{0,2,1:T(8,128)(2,1)S(1)}, bf16[1024,4,32]{0,2,1:T(8,128)(2,1)}, u32[]{:S(2)}) copy-start(bf16[1024,4,32]{0,2,1:T(8,128)(2,1)} %copy-done.5) | copy-start | bytes 786436
  457.3 5.7 %copy-start.8 = (bf16[1024,4,32]{0,2,1:T(8,128)(2,1)S(1)}, bf16[1024,4,32]{0,2,1:T(8,128)(2,1)}, u32[]{:S(2)}) copy-start(bf16[1024,4,32]{0,2,1:T(8,128)(2,1)} %copy-done.7) | copy-start | bytes 786436
  463.1 3.4 copy-start.2
  463.1 35.1 %copy-start.3 = (bf16[128,2304]{1,0:T(8,128)(2,1)S(1)}, bf16[128,2304]{1,0:T(8,128)(2,1)}, u32[]{:S(2)}) copy-start(bf16[128,2304]{1,0:T(8,128)(2,1)} %reduce-scatter.3.cloned.1.call-done) | copy-start | bytes 1769476
  463.1 37.3 %copy-start.4 = (bf16[256,2304]{1,0:T(8,128)(2,1)S(1)}, bf16[256,2304]{1,0:T(8,128)(2,1)}, u32[]{:S(2)}) copy-start(bf16[256,2304]{1,0:T(8,128)(2,1)} %all-gather.7.cloned.1.call-done) | copy-start | bytes 3538948
Sparse Core Ops, SparseCore 0:
  42.0 69.6 all-gather.4
  114.2 37.5 all-gather.8
  153.9 30.4 all-gather.6
  189.4 52.9 reduce-scatter.2
  246.1 60.3 all-gather.10
  445.1 53.0 reduce-scatter.4
where the time goes:
time: 513 us; the launch traced here: 509 us
  waiting for transfers between devices  279 us (54%)
  local copies, waits for them, and re-layouts  91.6 us (18%)
  other arithmetic  47.8 us (9%)
  matrix products  40.3 us (8%)
  blocking collectives  18.9 us (4%)
  between operations  16 us (3%)
  starting transfers between devices  14.5 us (3%)
    all_gather x1, waiting for transfers between devices, shards(): lax.all_gather(column_part, 'dp', axis=0, tiled=True)  65.7 us
    reduce_scatter x1, waiting for transfers between devices, shards(): lax.psum_scatter(jnp.dot(attended, server_out, preferred_element_type=jnp...  52.6 us
    all_gather x1, waiting for transfers between devices, shards(): piece = lax.all_gather(normed, 'tensor', axis=0, tiled=True)  35.8 us
    all_to_all x1, waiting for transfers between devices, shards(): lax.all_to_all(trainer_gate.astype(jnp.bfloat16), 'tensor', split_axis=1,...  35.8 us
    reduce_scatter x1, waiting for transfers between devices, shards(): lax.psum_scatter(terms.astype(jnp.bfloat16), 'tensor', scatter_dimension=...  31.4 us
    unnamed x35, local copies, waits for them, and re-layouts  30.7 us
    all_to_all x1, waiting for transfers between devices, shards(): lax.all_to_all(trainer_up.astype(jnp.bfloat16), 'tensor', split_axis=1, c...  24.2 us
    all_to_all x1, waiting for transfers between devices, shards(): lax.all_to_all(trainer_down.astype(jnp.bfloat16), 'tensor', split_axis=1,...  24 us
  transfers between devices with their start and end apart: 9, of which 8 were waited for; matrix products, arithmetic and copies ran while one was open for 19% of the time, Pallas kernels for 0%

commit v1 on v0

--- a/solution.py
+++ b/solution.py
@@ -4,6 +4,28 @@
 from jax.sharding import PartitionSpec as P
 
 HEAD_DIM = 64
+
+
+def laid_out(parts, dim):
+    lengths = list(parts.shape[1:])
+    lengths[dim] *= parts.shape[0]
+    return jnp.moveaxis(parts, 0, dim).reshape(lengths)
+
+
+def ring_gather(x, axis, dim):
+    length = lax.axis_size(axis)
+    pairs = [(i, (i + 1) % length) for i in range(length)]
+    back = [(b, a) for a, b in pairs]
+    lower, upper = ([], [])
+    for hop in range(length - 1):
+        if hop % 2 == 0:
+            lower.append(lax.ppermute(lower[-1] if lower else x, axis, pairs))
+        else:
+            upper.append(lax.ppermute(upper[-1] if upper else x, axis, back))
+    parts = jnp.stack([*lower[::-1], x, *upper])
+    shift = lax.axis_index(axis) - len(lower)
+    parts = parts[(jnp.arange(length) - shift) % length]
+    return laid_out(parts, dim)
 
 
 def rms_scale(values, gain_row):
@@ -95,7 +117,7 @@
     normed = rms_scale(tokens, attn_gain).astype(jnp.bfloat16)
     local_width = server_qkv.shape[2]
     heads_here = local_width // HEAD_DIM
-    piece = lax.all_gather(normed, "tensor", axis=0, tiled=True)
+    piece = ring_gather(normed, "tensor", 0)
     mixed = jnp.einsum("sd,dtc->stc", piece, server_qkv, preferred_element_type=jnp.float32)
     places = offset + jnp.arange(piece.shape[0], dtype=jnp.int32)
     query_rot = rotate(mixed[:, 0].reshape(-1, heads_here, HEAD_DIM), places).reshape(

time: 513 us -> 473 us (0.922)
  waiting for transfers between devices: 279 us -> 216 us
  local copies, waits for them, and re-layouts: 91.6 us -> 104 us
  starting transfers between devices: 14.5 us -> 22.5 us
    all_gather x1, waiting for transfers between devices: 65.7 us -> 0.01 us  [shards(): lax.all_gather(column_part, 'dp', axis=0, tiled=True)]
    ppermute x0 -> x7, waiting for transfers between devices: none -> 46 us  [the longest x4 46 us: ring_gather(): lower.append(lax.ppermute(lower[-1] if lower else x, axis, pairs))]
    all_gather x1 -> x0, waiting for transfers between devices: 35.8 us -> none  [shards(): piece = lax.all_gather(normed, 'tensor', axis=0, tiled=True)]
    ppermute x0 -> x7, starting transfers between devices: none -> 8.33 us  [the longest x3 8.32 us: ring_gather(): upper.append(lax.ppermute(upper[-1] if upper else x, axis, back))]
    unnamed x35 -> x53, local copies, waits for them, and re-layouts: 30.7 us -> 38.5 us
    all_gather x1, waiting for transfers between devices: 9.96 us -> 2.3 us  [shards(): lax.all_gather(out_cast, 'dp', axis=0, tiled=True)]
    gather x0 -> x1, local copies, waits for them, and re-layouts: none -> 5.36 us  [ring_gather(): parts = parts[(jnp.arange(length) - shift) % length]]
  transfers between devices with their start and end apart: 9 -> 15, of which waited for: 8 -> 10; matrix products, arithmetic and copies ran while one was open for 19% -> 23% of each run, Pallas kernels for 0% -> 0%
where the time goes in v1:
time: 473 us; the launch traced here: 467 us
  waiting for transfers between devices  216 us (46%)
  local copies, waits for them, and re-layouts  104 us (22%)
  other arithmetic  50.9 us (11%)
  matrix products  38.5 us (8%)
  starting transfers between devices  22.5 us (5%)
  blocking collectives  18.9 us (4%)
  between operations  15.7 us (3%)
    reduce_scatter x1, waiting for transfers between devices, shards(): lax.psum_scatter(jnp.dot(attended, server_out, preferred_element_type=jnp...  52.6 us
    ppermute x4, waiting for transfers between devices, ring_gather(): lower.append(lax.ppermute(lower[-1] if lower else x, axis, pairs))  46 us
    unnamed x53, local copies, waits for them, and re-layouts  38.5 us
    all_to_all x1, waiting for transfers between devices, shards(): lax.all_to_all(trainer_gate.astype(jnp.bfloat16), 'tensor', split_axis=1,...  35.8 us
    reduce_scatter x1, waiting for transfers between devices, shards(): lax.psum_scatter(terms.astype(jnp.bfloat16), 'tensor', scatter_dimension=...  31.4 us
    all_to_all x1, waiting for transfers between devices, shards(): lax.all_to_all(trainer_up.astype(jnp.bfloat16), 'tensor', split_axis=1, c...  24.2 us
    all_to_all x1, waiting for transfers between devices, shards(): lax.all_to_all(trainer_down.astype(jnp.bfloat16), 'tensor', split_axis=1,...  24 us
    all_to_all x1, blocking collectives, shards(): lax.all_to_all(qkv_cast, 'tensor', split_axis=2, concat_axis=0, tiled=True)  18.9 us
  transfers between devices with their start and end apart: 15, of which 10 were waited for; matrix products, arithmetic and copies ran while one was open for 23% of the time, Pallas kernels for 0%

profile of v1, /device:TPU:0, one launch (start us, length us, event | category | flops | bytes accessed | tf_op | source)
XLA Modules:
  0.0 466.8 jit_solution(15358737412848456474)
XLA Ops:
  7.2 2.5 convert_element_type.92
  9.7 2.9 copy.59
  12.6 3.7 reshape.345
  16.3 18.9 %all_to_all.75 = bf16[8,2,27648]{2,1,0:T(2,128)(2,1)} all-to-all(bf16[8,2,27648]{2,1,0:T(2,128)(2,1)} %reshape.345), channel_id=1, replica_groups=mesh['dp'=4,'tensor'=8] {'tensor'}, dimensions={0} | all-to-all | bytes 1769472 | tf_op jit(solution)/shard_map/all_to_all | solution.py:100
  35.2 4.5 reshape.346
  43.2 10.4 %collective-permute-done = bf16[128,2304]{1,0:T(8,128)(2,1)S(1)} collective-permute-done((bf16[128,2304]{1,0:T(8,128)(2,1)}, bf16[128,2304]{1,0:T(8,128)(2,1)S(1)}, u32[]{:S(2)}, u32[]{:S(2)}) %collective-permute-start) | collective-permute-done | bytes 589856 | tf_op jit(solution)/shard_map/ppermute | solution.py:22
  53.6 2.6 collective-permute-start.4
  56.3 13.2 %collective-permute-done.1 = bf16[128,2304]{1,0:T(8,128)(2,1)S(1)} collective-permute-done((bf16[128,2304]{1,0:T(8,128)(2,1)S(1)}, bf16[128,2304]{1,0:T(8,128)(2,1)S(1)}, u32[]{:S(2)}, u32[]{:S(2)}) %collective-permute-start.1) | collective-permute-done | bytes 589856 | tf_op jit(solution)/shard_map/ppermute | solution.py:22
  71.0 2.7 collective-permute-start.5
  73.7 11.3 %collective-permute-done.2 = bf16[128,2304]{1,0:T(8,128)(2,1)} collective-permute-done((bf16[128,2304]{1,0:T(8,128)(2,1)S(1)}, bf16[128,2304]{1,0:T(8,128)(2,1)}, u32[]{:S(2)}, u32[]{:S(2)}) %collective-permute-start.2) | collective-permute-done | bytes 589856 | tf_op jit(solution)/shard_map/ppermute | solution.py:22
  87.4 3.0 collective-permute-start.6
  90.4 11.1 %collective-permute-done.3 = bf16[128,2304]{1,0:T(8,128)(2,1)S(1)} collective-permute-done((bf16[128,2304]{1,0:T(8,128)(2,1)}, bf16[128,2304]{1,0:T(8,128)(2,1)S(1)}, u32[]{:S(2)}, u32[]{:S(2)}) %collective-permute-start.3) | collective-permute-done | bytes 589856 | tf_op jit(solution)/shard_map/ppermute | solution.py:22
  109.6 5.4 %gather_fusion = bf16[8,128,2304]{2,1,0:T(8,128)(2,1)} fusion(bf16[8,128,2304]{2,1,0:T(8,128)(2,1)} %bitcast_dynamic-update-slice_fusion, s32[1024]{0:T(1024)S(1)} %pad_clamp_fusion.1), kind=kCustom, calls=%fused_computation | custom fusion | bytes 9437216 | tf_op jit(solution)/shard_map/gather | solution.py:27
  115.0 2.5 copy.62
  118.4 4.0 fusion.67
  124.4 4.8 %fusion.69 = (f32[4,512]{1,0:T(4,128)S(1)}, f32[4,512,512]{1,2,0:T(8,128)}) fusion(pred[512,512]{0,1:T(8,128)(4,1)S(1)} %copy-done.14, bf16[1024,4,32]{0,2,1:T(8,128)(2,1)S(1)} %get-tuple-element.48, bf16[1024,4,32]{0,2,1:T(8,128)(2,1)S(1)} %get-tuple-element.49, bf16[1024,4,32]{0,2,1:T(8,128)(2,1)} %get-tuple-element.53, ...), kind=kOutput, calls=%fused_computation.128 | convolution fusion | flops 139461120 | bytes 5513216 | tf_op jit(solution)/shard_map/sub | solution.py:63
  129.1 5.4 %fusion.68 = (f32[4,512]{1,0:T(4,128)S(1)}, f32[4,512,1024]{2,1,0:T(8,128)}) fusion(pred[512,1024]{1,0:T(8,128)(4,1)S(1)} %iota_compare_fusion, bf16[1024,4,32]{0,2,1:T(8,128)(2,1)S(1)} %get-tuple-element.52, bf16[1024,4,32]{0,2,1:T(8,128)(2,1)S(1)} %copy-done.15, bf16[1024,4,32]{0,2,1:T(8,128)(2,1)S(1)} %get-tuple-element.49, ...), kind=kOutput, calls=%fused_computation.127 | convolution fusion | flops 278397952 | bytes 9969664 | tf_op jit(solution)/shard_map/sub | solution.py:63
  134.5 2.9 fusion.31
  140.7 2.3 all-gather.6.cloned.1.call-done
  143.0 4.9 %convolution_convert_fusion = bf16[1024,2304]{1,0:T(8,128)(2,1)} fusion(bf16[1024,256]{0,1:T(8,128)(2,1)S(1)} %bitcast.133, bf16[256,2304]{1,0:T(8,128)(2,1)} %all-gather.6.cloned.1.call-done), kind=kOutput, calls=%fused_computation.10 | convolution fusion | flops 1210318848 | bytes 6422528 | tf_op jit(solution)/shard_map/dot_general | solution.py:143
  148.5 52.6 %reduce-scatter.3.cloned.1.call-done = bf16[128,2304]{1,0:T(8,128)(2,1)} async-done(((bf16[1024,2304]{1,0:T(8,128)(2,1)}), bf16[128,2304]{1,0:T(8,128)(2,1)}) %reduce-scatter.3.cloned.1.call-update) | async-done | bytes 589840 | tf_op jit(solution)/shard_map/reduce_scatter | solution.py:142
  204.6 4.9 %convert_element_type.94 = bf16[288,5760]{1,0:T(8,128)(2,1)} convert(f32[288,5760]{1,0:T(8,128)} %param.18) | non-fusion elementwise | flops 1658880 | bytes 9953280 | tf_op jit(solution)/shard_map/convert_element_type | solution.py:88
  209.5 8.6 %all_to_all.59 = bf16[288,8,720]{2,1,0:T(8,128)(2,1)} reshape(bf16[288,5760]{1,0:T(8,128)(2,1)} %convert_element_type.94) | data formatting | bytes 6635520 | tf_op jit(solution)/shard_map/all_to_all | solution.py:87
  218.1 4.5 copy.63
  222.6 4.5 all-to-all-start.1
  227.1 5.0 %convert_element_type.95 = bf16[288,5760]{1,0:T(8,128)(2,1)} convert(f32[288,5760]{1,0:T(8,128)} %param.19) | non-fusion elementwise | flops 1658880 | bytes 9953280 | tf_op jit(solution)/shard_map/convert_element_type | solution.py:91
  232.1 8.5 %all_to_all.63 = bf16[288,8,720]{2,1,0:T(8,128)(2,1)} reshape(bf16[288,5760]{1,0:T(8,128)(2,1)} %convert_element_type.95) | data formatting | bytes 6635520 | tf_op jit(solution)/shard_map/all_to_all | solution.py:90
  240.6 4.5 copy.64
  245.0 35.8 %all-to-all-done.1 = bf16[288,8,720]{2,0,1:T(8,128)(2,1)} async-done(((bf16[288,8,720]{2,0,1:T(8,128)(2,1)}), bf16[288,8,720]{2,0,1:T(8,128)(2,1)}, u32[]{:S(2)}, u32[]{:S(2)}) %all-to-all-start.1) | async-done | bytes 3317792 | tf_op jit(solution)/shard_map/all_to_all | solution.py:87
  280.8 4.5 all-to-all-start.2
  285.3 4.9 %convert_element_type.96 = bf16[288,5760]{1,0:T(8,128)(2,1)} convert(f32[288,5760]{1,0:T(8,128)} %param.20) | non-fusion elementwise | flops 1658880 | bytes 9953280 | tf_op jit(solution)/shard_map/convert_element_type | solution.py:94
  290.3 8.5 %all_to_all.67 = bf16[288,8,720]{2,1,0:T(8,128)(2,1)} reshape(bf16[288,5760]{1,0:T(8,128)(2,1)} %convert_element_type.96) | data formatting | bytes 6635520 | tf_op jit(solution)/shard_map/all_to_all | solution.py:93
  298.7 4.5 copy.65
  303.3 24.2 %all-to-all-done.2 = bf16[288,8,720]{2,0,1:T(8,128)(2,1)} async-done(((bf16[288,8,720]{2,0,1:T(8,128)(2,1)}), bf16[288,8,720]{2,0,1:T(8,128)(2,1)}, u32[]{:S(2)}, u32[]{:S(2)}) %all-to-all-start.2) | async-done | bytes 3317792 | tf_op jit(solution)/shard_map/all_to_all | solution.py:90
  327.4 4.5 all-to-all-start.3
  332.6 4.5 scatter_custom_fusion
  337.2 7.8 %gather_fusion.1 = bf16[512,2304]{1,0:T(8,128)(2,1)S(1)} fusion(bf16[1024,2304]{1,0:T(8,128)(2,1)} %all-gather.8.cloned.1.call-done, s32[1024]{0:T(1024)S(1)} %pad_clamp_fusion), kind=kCustom, calls=%fused_computation.1 | custom fusion | bytes 4720640 | tf_op jit(solution)/shard_map/gather | solution.py:173
  345.0 5.0 %fusion.78 = f32[512,720]{0,1:T(8,128)} fusion(bf16[512,2304]{1,0:T(8,128)(2,1)S(1)} %gather_fusion.1, bf16[2304,720]{1,0:T(8,128)(2,1)} %bitcast.8), kind=kOutput, calls=%fused_computation.129 | convolution fusion | flops 1698693120 | bytes 7151616 | tf_op jit(solution)/shard_map/dot_general | solution.py:174
  350.1 24.0 %all-to-all-done.3 = bf16[288,8,720]{2,0,1:T(8,128)(2,1)} async-done(((bf16[288,8,720]{2,0,1:T(8,128)(2,1)}), bf16[288,8,720]{2,0,1:T(8,128)(2,1)}, u32[]{:S(2)}, u32[]{:S(2)}) %all-to-all-start.3) | async-done | bytes 3317792 | tf_op jit(solution)/shard_map/all_to_all | solution.py:93
  374.0 9.9 %fusion.35 = f32[512,2304]{1,0:T(8,128)} fusion(bf16[2304,720]{1,0:T(8,128)(2,1)} %bitcast.12, f32[512,720]{0,1:T(8,128)} %fusion.78, bf16[512,2304]{1,0:T(8,128)(2,1)S(1)} %gather_fusion.1, bf16[2304,720]{1,0:T(8,128)(2,1)} %bitcast.10), kind=kOutput, calls=%fused_computation.54 | convolution fusion | flops 3399598080 | bytes 15187968 | tf_op jit(solution)/shard_map/dot_general | solution.py:177
  384.0 13.3 %scatter_custom_fusion.1 = f32[1024,2304]{1,0:T(8,128)} fusion(s32[512]{0:T(512)S(1)} %get-tuple-element.57, f32[512,2304]{1,0:T(8,128)} %fusion.35, f32[]{:T(128)} %constant.23.clone.1), kind=kCustom, calls=%fused_computation.11 | custom fusion | flops 1179648 | bytes 9437696 | tf_op jit(solution)/shard_map/scatter-add | solution.py:183
  397.2 6.4 %convert_element_type.117 = bf16[1024,2304]{1,0:T(8,128)(2,1)} convert(f32[1024,2304]{1,0:T(8,128)} %scatter_custom_fusion.1) | non-fusion elementwise | flops 2359296 | bytes 14155776 | tf_op jit(solution)/shard_map/convert_element_type | solution.py:186
  404.3 5.7 %copy.68 = bf16[2304,720]{0,1:T(8,128)(2,1)} copy(bf16[2304,720]{1,0:T(8,128)(2,1)} %bitcast.8) | data formatting | bytes 6635520
  410.0 5.9 %copy.69 = bf16[2304,720]{0,1:T(8,128)(2,1)} copy(bf16[2304,720]{1,0:T(8,128)(2,1)} %bitcast.10) | data formatting | bytes 6635520
  416.0 5.7 %copy.70 = bf16[2304,720]{0,1:T(8,128)(2,1)} copy(bf16[2304,720]{1,0:T(8,128)(2,1)} %bitcast.12) | data formatting | bytes 6635520
  422.9 2.3 copy.71
  425.4 31.4 %reduce-scatter.5.cloned.1.call-done = bf16[128,2304]{1,0:T(8,128)(2,1)} async-done(((bf16[1024,2304]{1,0:T(8,128)(2,1)}), bf16[128,2304]{1,0:T(8,128)(2,1)}) %reduce-scatter.5.cloned.1.call-update) | async-done | bytes 589840 | tf_op jit(solution)/shard_map/reduce_scatter | solution.py:185
  456.8 2.2 fusion.36
  (109 shorter events, 28.4 us)
Async XLA Ops:
  7.2 418.0 %copy-start = (bf16[2304,8]{0,1:T(8,128)(2,1)S(1)}, bf16[2304,8]{0,1:T(8,128)(2,1)}, u32[]{:S(2)}) copy-start(bf16[2304,8]{0,1:T(8,128)(2,1)} %param.23) | copy-start | bytes 110596
  7.2 107.8 %all-gather.4.cloned.1.call-start = ((), (), s32[]{:S(2)}) async-start(), calls=%async_computation.6 | async-start | bytes 4423680 | tf_op jit(solution)/shard_map/all_gather | solution.py:102
  35.2 6.8 %copy-start.1 = (bf16[1,128,2304]{2,1,0:T(8,128)(2,1)S(1)}, bf16[1,128,2304]{2,1,0:T(8,128)(2,1)}, u32[]{:S(2)}) copy-start(bf16[1,128,2304]{2,1,0:T(8,128)(2,1)} %param.12) | copy-start | bytes 1769476
  35.2 7.0 %copy-start.16 = (f32[2304]{0:T(1024)S(1)}, f32[2304]{0:T(1024)}, u32[]{:S(2)}) copy-start(f32[2304]{0:T(1024)} %param.21) | copy-start | bytes 27652
  39.7 29.8 %copy-start.11 = (f32[64,2304]{1,0:T(8,128)S(1)}, f32[64,2304]{1,0:T(8,128)}, u32[]{:S(2)}) copy-start(f32[64,2304]{1,0:T(8,128)} %param.17) | copy-start | bytes 1769476
  41.9 101.1 %all-gather.6.cloned.1.call-start = ((), (), s32[]{:S(2)}) async-start(), calls=%async_computation.7 | async-start | bytes 1474560 | tf_op jit(solution)/shard_map/all_gather | solution.py:103
  43.2 10.4 %collective-permute-start = (bf16[128,2304]{1,0:T(8,128)(2,1)}, bf16[128,2304]{1,0:T(8,128)(2,1)S(1)}, u32[]{:S(2)}, u32[]{:S(2)}) collective-permute-start(bf16[128,2304]{1,0:T(8,128)(2,1)} %fusion.21), channel_id=1, source_target_pairs={{0,1},{1,2},{2,3},{3,4},{4,5},{5,6},{6,7},{7,0},{8,9},{9,10},{10,1... | collective-permute-start | bytes 1769480 | tf_op jit(solution)/shard_map/ppermute | solution.py:22
  53.6 15.8 %collective-permute-start.1 = (bf16[128,2304]{1,0:T(8,128)(2,1)S(1)}, bf16[128,2304]{1,0:T(8,128)(2,1)S(1)}, u32[]{:S(2)}, u32[]{:S(2)}) collective-permute-start(bf16[128,2304]{1,0:T(8,128)(2,1)S(1)} %collective-permute-done), channel_id=1, source_target_pairs={{0,1},{1,2},{2,3},{3,4},{4,5},{5,6},{6,7},{7,0},{8,9},{9,10},{10,1... | collective-permute-start | bytes 1769480 | tf_op jit(solution)/shard_map/ppermute | solution.py:22
  53.6 17.3 %collective-permute-start.4 = (bf16[128,2304]{1,0:T(8,128)(2,1)}, bf16[128,2304]{1,0:T(8,128)(2,1)S(1)}, u32[]{:S(2)}, u32[]{:S(2)}) collective-permute-start(bf16[128,2304]{1,0:T(8,128)(2,1)} %fusion.21), channel_id=1, source_target_pairs={{1,0},{2,1},{3,2},{4,3},{5,4},{6,5},{7,6},{0,7},{9,8},{10,9},{11,1... | collective-permute-start | bytes 1769480 | tf_op jit(solution)/shard_map/ppermute | solution.py:24
  69.4 15.5 %collective-permute-start.2 = (bf16[128,2304]{1,0:T(8,128)(2,1)S(1)}, bf16[128,2304]{1,0:T(8,128)(2,1)}, u32[]{:S(2)}, u32[]{:S(2)}) collective-permute-start(bf16[128,2304]{1,0:T(8,128)(2,1)S(1)} %collective-permute-done.1), channel_id=1, source_target_pairs={{0,1},{1,2},{2,3},{3,4},{4,5},{5,6},{6,7},{7,0},{8,9},{9,10},{10,1... | collective-permute-start | bytes 1769480 | tf_op jit(solution)/shard_map/ppermute | solution.py:22
  70.2 130.9 %reduce-scatter.3.cloned.1.call-start = ((), (), s32[]{:S(2)}) async-start(), calls=%async_computation.8 | async-start | bytes 5308416 | tf_op jit(solution)/shard_map/reduce_scatter | solution.py:142
  71.0 16.4 %collective-permute-start.5 = (bf16[128,2304]{1,0:T(8,128)(2,1)S(1)}, bf16[128,2304]{1,0:T(8,128)(2,1)S(1)}, u32[]{:S(2)}, u32[]{:S(2)}) collective-permute-start(bf16[128,2304]{1,0:T(8,128)(2,1)S(1)} %collective-permute-done.4), channel_id=1, source_target_pairs={{1,0},{2,1},{3,2},{4,3},{5,4},{6,5},{7,6},{0,7},{9,8},{10,9},{11,1... | collective-permute-start | bytes 1769480 | tf_op jit(solution)/shard_map/ppermute | solution.py:24
  85.0 16.5 %collective-permute-start.3 = (bf16[128,2304]{1,0:T(8,128)(2,1)}, bf16[128,2304]{1,0:T(8,128)(2,1)S(1)}, u32[]{:S(2)}, u32[]{:S(2)}) collective-permute-start(bf16[128,2304]{1,0:T(8,128)(2,1)} %collective-permute-done.2), channel_id=1, source_target_pairs={{0,1},{1,2},{2,3},{3,4},{4,5},{5,6},{6,7},{7,0},{8,9},{9,10},{10,1... | collective-permute-start | bytes 1769480 | tf_op jit(solution)/shard_map/ppermute | solution.py:22
  87.4 21.4 %collective-permute-start.6 = (bf16[128,2304]{1,0:T(8,128)(2,1)S(1)}, bf16[128,2304]{1,0:T(8,128)(2,1)S(1)}, u32[]{:S(2)}, u32[]{:S(2)}) collective-permute-start(bf16[128,2304]{1,0:T(8,128)(2,1)S(1)} %collective-permute-done.5), channel_id=1, source_target_pairs={{1,0},{2,1},{3,2},{4,3},{5,4},{6,5},{7,6},{0,7},{9,8},{10,9},{11,1... | collective-permute-start | bytes 1769480 | tf_op jit(solution)/shard_map/ppermute | solution.py:24
  115.0 3.4 copy-start.5
  117.5 4.8 %copy-start.6 = (bf16[8,4,72,3,256]{4,2,1,0,3:T(8,128)(2,1)}, bf16[8,4,72,3,256]{4,2,1,0,3:T(8,128)(2,1)S(1)}, u32[]{:S(2)}) copy-start(bf16[8,4,72,3,256]{4,2,1,0,3:T(8,128)(2,1)S(1)} %copy.62) | copy-start | bytes 10616836
  122.3 0.9 copy-start.12
  122.4 1.0 copy-start.13
  122.4 1.9 copy-start.14
  124.3 4.8 %copy-start.7 = (bf16[1024,4,32]{0,2,1:T(8,128)(2,1)}, bf16[1024,4,32]{0,2,1:T(8,128)(2,1)S(1)}, u32[]{:S(2)}) copy-start(bf16[1024,4,32]{0,2,1:T(8,128)(2,1)S(1)} %get-tuple-element.48) | copy-start | bytes 786436
  124.3 4.8 %copy-start.9 = (bf16[1024,4,32]{0,2,1:T(8,128)(2,1)}, bf16[1024,4,32]{0,2,1:T(8,128)(2,1)S(1)}, u32[]{:S(2)}) copy-start(bf16[1024,4,32]{0,2,1:T(8,128)(2,1)S(1)} %get-tuple-element.49) | copy-start | bytes 786436
  124.3 4.8 %copy-start.15 = (bf16[1024,4,32]{0,2,1:T(8,128)(2,1)S(1)}, bf16[1024,4,32]{0,2,1:T(8,128)(2,1)}, u32[]{:S(2)}) copy-start(bf16[1024,4,32]{0,2,1:T(8,128)(2,1)} %get-tuple-element.53) | copy-start | bytes 786436
  134.5 4.7 %copy-start.19 = (f32[4,512,1024]{2,1,0:T(8,128)S(1)}, f32[4,512,1024]{2,1,0:T(8,128)}, u32[]{:S(2)}) copy-start(f32[4,512,1024]{2,1,0:T(8,128)} %get-tuple-element.63) | copy-start | bytes 25165828
  147.9 54.5 %copy-start.17 = (f32[2304]{0:T(1024)S(1)}, f32[2304]{0:T(1024)}, u32[]{:S(2)}) copy-start(f32[2304]{0:T(1024)} %param.22) | copy-start | bytes 27652
  147.9 189.3 %all-gather.8.cloned.1.call-start = ((), (), s32[]{:S(2)}) async-start(), calls=%async_computation.9 | async-start | bytes 5308416 | tf_op jit(solution)/shard_map/all_gather | solution.py:163
  222.6 58.2 %all-to-all-start.1 = ((bf16[288,8,720]{2,0,1:T(8,128)(2,1)}), bf16[288,8,720]{2,0,1:T(8,128)(2,1)}, u32[]{:S(2)}, u32[]{:S(2)}) async-start(bf16[288,8,720]{2,0,1:T(8,128)(2,1)} %copy.63), calls=%async_computation.1 | async-start | bytes 7077888 | tf_op jit(solution)/shard_map/all_to_all | solution.py:87
  280.8 46.6 %all-to-all-start.2 = ((bf16[288,8,720]{2,0,1:T(8,128)(2,1)}), bf16[288,8,720]{2,0,1:T(8,128)(2,1)}, u32[]{:S(2)}, u32[]{:S(2)}) async-start(bf16[288,8,720]{2,0,1:T(8,128)(2,1)} %copy.64), calls=%async_computation.2 | async-start | bytes 7077888 | tf_op jit(solution)/shard_map/all_to_all | solution.py:90
  303.3 28.7 %copy-start.18 = (s32[1,1024,2]{1,2,0:T(2,128)S(1)}, s32[1,1024,2]{1,2,0:T(2,128)}, u32[]{:S(2)}) copy-start(s32[1,1024,2]{1,2,0:T(2,128)} %param.15) | copy-start | bytes 24580
  327.4 46.6 %all-to-all-start.3 = ((bf16[288,8,720]{2,0,1:T(8,128)(2,1)}), bf16[288,8,720]{2,0,1:T(8,128)(2,1)}, u32[]{:S(2)}, u32[]{:S(2)}) async-start(bf16[288,8,720]{2,0,1:T(8,128)(2,1)} %copy.65), calls=%async_computation.3 | async-start | bytes 7077888 | tf_op jit(solution)/shard_map/all_to_all | solution.py:93
  331.9 124.9 %reduce-scatter.5.cloned.1.call-start = ((), (), s32[]{:S(2)}) async-start(), calls=%async_computation.10 | async-start | bytes 5308416 | tf_op jit(solution)/shard_map/reduce_scatter | solution.py:185
  416.0 5.7 %copy-start.8 = (bf16[1024,4,32]{0,2,1:T(8,128)(2,1)S(1)}, bf16[1024,4,32]{0,2,1:T(8,128)(2,1)}, u32[]{:S(2)}) copy-start(bf16[1024,4,32]{0,2,1:T(8,128)(2,1)} %copy-done.7) | copy-start | bytes 786436
  416.0 5.7 %copy-start.10 = (bf16[1024,4,32]{0,2,1:T(8,128)(2,1)S(1)}, bf16[1024,4,32]{0,2,1:T(8,128)(2,1)}, u32[]{:S(2)}) copy-start(bf16[1024,4,32]{0,2,1:T(8,128)(2,1)} %copy-done.9) | copy-start | bytes 786436
  421.7 3.4 copy-start.2
  421.7 35.1 %copy-start.3 = (bf16[128,2304]{1,0:T(8,128)(2,1)S(1)}, bf16[128,2304]{1,0:T(8,128)(2,1)}, u32[]{:S(2)}) copy-start(bf16[128,2304]{1,0:T(8,128)(2,1)} %reduce-scatter.3.cloned.1.call-done) | copy-start | bytes 1769476
  421.8 37.3 %copy-start.4 = (bf16[256,2304]{1,0:T(8,128)(2,1)S(1)}, bf16[256,2304]{1,0:T(8,128)(2,1)}, u32[]{:S(2)}) copy-start(bf16[256,2304]{1,0:T(8,128)(2,1)} %all-gather.6.cloned.1.call-done) | copy-start | bytes 3538948
Sparse Core Ops, SparseCore 0:
  42.0 69.7 all-gather.3
  113.9 29.0 all-gather.5
  148.0 52.9 reduce-scatter.2
  204.7 60.3 all-gather.7
  403.8 53.0 reduce-scatter.4
